TPU v7x, 32 devices: a whole 2x2x4 slice. The times are simulated.
32 devices in a mesh: tx: 4 (over x, core), py: 2 (over y), pz: 4 (over z).
Axes of the slice: x: 2, y: 2, z: 4, core: 2. Of those that a mesh axis runs over, the one named last changes fastest.
Arguments:
- fields: float32 [16, 2, 128, 128, 128], P('tx', None, 'py', 'pz'), may hold values from 0.5 to 1.5
- sources: float32 [16, 2, 128, 128, 128], P('tx', None, 'py', 'pz'), may hold values from -12 to 12
- green: float32 [2, 128, 128, 128], P(None, 'pz', 'py'), may hold values from -6 to 6
Outputs:
- contrast_fine: float32 [2, 256, 256, 256], P(None, 'py', 'pz')
- scattered: float32 [4, 2, 256, 256, 256], P('tx', None, 'py', 'pz')
All inputs are finite; a program needn't handle non-finite values.
Results may differ from a plain program's by a relative error of at most 0.00014.
Values sent between devices are 32-bit elements; how exact they have to be, the bound alone decides.
A program may use at most 192 MiB of HBM per device.

v0:
```python
import functools
import math

import jax
import jax.numpy as jnp
import ml_dtypes
import numpy as np
from jax import lax
from jax.experimental import pallas as pl
from jax.experimental.pallas import tpu as pltpu
from jax.sharding import PartitionSpec as P

F32 = jnp.float32
BF16 = jnp.bfloat16
NN = (((1,), (0,)), ((), ()))
NT = (((1,), (1,)), ((), ()))
MESH = pl.DeviceIdType.MESH
ROWS = 8
GROUPS = 4
PARTS = 4


def signed(count):
    index = np.arange(count)
    return np.where(index < count // 2, index, index - count)


def forward_matrix(coarse):
    index = np.arange(coarse)
    return np.exp(-2j * np.pi * ((index[:, None] * index[None, :]) % coarse) / coarse)


def inverse_matrix(coarse, fine):
    phases = (np.arange(fine)[:, None] * signed(coarse)[None, :]) % fine
    return np.exp(2j * np.pi * phases / fine) / coarse


def block_form(matrix):
    re, im = matrix.real, matrix.imag
    return np.stack([np.stack([re, -im], 1), np.stack([im, re], 1)], 0)


def halves(matrix):
    high = matrix.astype(ml_dtypes.bfloat16)
    low = (matrix - high.astype(np.float64)).astype(ml_dtypes.bfloat16)
    return high, low


def left_table(matrix):
    high, low = halves(matrix)
    return jnp.asarray(np.concatenate([high, high, low], axis=-1))


def right_table(matrix):
    high, low = halves(matrix)
    return jnp.asarray(np.concatenate([high, high, low], axis=-2))


def split(x):
    high = x.astype(BF16)
    return high, (x - high.astype(F32)).astype(BF16)


def product_left(m, x, dims=NN):
    high, low = split(x)
    axis = dims[0][1][0]
    wide = jnp.concatenate([high, low, high], axis=axis)
    return lax.dot_general(m, wide, dimension_numbers=dims, preferred_element_type=F32)


def product_right(x, m):
    high, low = split(x)
    wide = jnp.concatenate([high, low, high], axis=1)
    return lax.dot_general(wide, m, dimension_numbers=NN, preferred_element_type=F32)


def times_i(x):
    half = x.shape[1] // 2
    return jnp.concatenate([-x[:, half:], x[:, :half]], axis=1)


def flip(me, bit):
    return me + bit - 2 * bit * ((me // bit) % 2)


def flips(me, code):
    for bit in (1, 2):
        if code & bit:
            me = flip(me, bit)
    return me


def remote(src, dst, sends, recvs, where):
    return pltpu.make_async_remote_copy(
        src_ref=src, dst_ref=dst, send_sem=sends, recv_sem=recvs,
        device_id=where, device_id_type=MESH,
    )


def exchange_body(
    fields, sources, green, h_s1, h_top, h_f2, h_inv, h_first, h_mid, h_fc,
    ts_out, tc_out,
    xs, s1, yr, s2, zr, gb, s4, fin, fb, sb, sums, cr, xr, cz, cg, st,
    w_s1, w_top, w_f2, w_inv, w_first, w_mid, w_fc,
    load_sem, step_sem, out_sem, local_sem,
    y_s, y_r, z_s, z_r, g_s, g_r, core_s, core_r, x_s, x_r, zc_s, zc_r,
    cy_s, cy_r, cx_s, cx_r, cc_s, cc_r, zb_s, zb_r, yh_s, yh_r,
):
    t, y, z = lax.axis_index("tx"), lax.axis_index("py"), lax.axis_index("pz")
    oy = 1 - y
    z_peer = [flips(z, j) for j in (1, 2, 3)]
    to_z = [{"pz": p} for p in z_peer]
    to_y = {"py": oy}
    core, far = flip(t, 1), flip(t, 2)
    to_core, to_x = {"tx": core}, {"tx": far}
    x_chunks = xs.shape[0]
    k_own = gb.shape[1]
    part = sums.shape[2]
    f_chunks = fin.shape[0]
    rows_h = part // PARTS
    lanes = s1.shape[5]
    coarse = green.shape[3]
    f1 = st.shape[1]

    loads = [
        pltpu.make_async_copy(sources.at[0, :, :, pl.ds(c * ROWS, ROWS), :], xs.at[c], load_sem.at[c])
        for c in range(x_chunks)
    ]
    tables = [
        pltpu.make_async_copy(src, dst, load_sem.at[x_chunks + i])
        for i, (src, dst) in enumerate(
            [
                (h_s1, w_s1), (h_top.at[y], w_top), (h_f2, w_f2), (h_inv, w_inv),
                (h_mid.at[z], w_mid), (h_first.at[y], w_first), (h_fc.at[y], w_fc),
                (green.at[:, pl.ds(y * k_own, k_own)], gb.at[:, :, y]),
            ]
        )
    ]
    order = (1, 3, 0, 2)
    per_block = part // ROWS

    def step_copies(i):
        row = flips(t, order[i // per_block]) * part + (i % per_block) * ROWS
        at = pl.ds(row, ROWS)
        slot = i % 2
        return (
            pltpu.make_async_copy(fields.at[:, :, at], fb.at[slot], step_sem.at[0, slot]),
            pltpu.make_async_copy(sources.at[:, :, at], sb.at[slot], step_sem.at[1, slot]),
        )

    tables[0].start()
    for c in loads:
        c.start()
    tables[1].start()
    for i in range(2):
        for c in step_copies(i):
            c.start()
    for c in tables[2:]:
        c.start()

    barrier = pltpu.get_barrier_semaphore()
    peers = to_z + [to_y, to_core, to_x]
    for where in peers:
        pl.semaphore_signal(barrier, inc=1, device_id=where, device_id_type=MESH)
    pl.semaphore_wait(barrier, len(peers))

    tables[0].wait()
    for c in loads:
        c.wait()

    def depth(c, _):
        for s in range(ROWS):
            re, im = xs[c, 0, :, s, :], xs[c, 1, :, s, :]
            both = jnp.concatenate(
                [jnp.concatenate([re, -im], axis=1), jnp.concatenate([im, re], axis=1)], axis=0
            )
            out = product_left(w_s1[...], both, NT)
            s1[:, :, :, c, s, :] = out.reshape(s1.shape[0], s1.shape[1], s1.shape[2], lanes)
        return 0

    lax.fori_loop(0, x_chunks, depth, 0)

    y_copies = [remote(s1.at[oy, g], yr.at[g], y_s.at[g], y_r.at[g], to_y) for g in range(GROUPS)]
    for c in y_copies:
        c.start()

    core_copies = [
        remote(sums.at[j], cr.at[n], core_s.at[n], core_r.at[n], to_core)
        for n, j in enumerate((1, 3))
    ]
    steps = len(order) * per_block

    def sum_step(i):
        slot, block, base = i % 2, order[i // per_block], (i % per_block) * ROWS
        for c in step_copies(i):
            c.wait()

        def row(r, _):
            total = None
            for k in range(fb.shape[1]):
                fr, fi = fb[slot, k, 0, r], fb[slot, k, 1, r]
                sr, si = sb[slot, k, 0, r], sb[slot, k, 1, r]
                term = (sr * fr + si * fi, si * fr - sr * fi, fr * fr + fi * fi)
                total = term if total is None else tuple(a + b for a, b in zip(total, term))
            for n in range(3):
                sums[block, n, base + r] = total[n]
            return 0

        lax.fori_loop(0, ROWS, row, 0)
        if i + 2 < steps:
            for c in step_copies(i + 2):
                c.start()

    def sum_block(b):
        for i in range(b * per_block, (b + 1) * per_block):
            sum_step(i)

    def z_copy(g, n):
        p = z_peer[n]
        return remote(s2.at[g, p], zr.at[g, :, z], z_s.at[g, n], z_r.at[g, n], to_z[n])

    def top(g):
        y_copies[g].wait_recv()
        rows = s1.shape[2] * s1.shape[3] * ROWS
        own = s1[y, g].reshape(rows, lanes)
        other = yr[g].reshape(rows, lanes)
        out = product_right(jnp.concatenate([own, other], axis=1), w_top[...])
        s2[g] = out.reshape(s2.shape[1:])
        for n in (2, 1, 0):
            z_copy(g, n).start()
        zr[g, :, z] = s2[g, z]

    sum_block(0)
    core_copies[0].start()
    sum_block(1)
    core_copies[1].start()
    tables[1].wait()
    top(0)
    green_copy = remote(
        green.at[:, pl.ds(oy * k_own, k_own)], gb.at[:, :, y], g_s.at[0], g_r.at[0], to_y
    )
    sum_block(2)
    sum_block(3)
    top(1)
    green_copy.start()
    for n, j in enumerate((0, 2)):
        core_copies[n].wait_recv()

        def add(r, _, n=n, j=j):
            for k in range(3):
                sums[j, k, r] = sums[j, k, r] + cr[n, k, r]
            return 0

        lax.fori_loop(0, part, add, 0)
    x_copies = []
    for h in range(PARTS):
        at = pl.ds(h * rows_h, rows_h)
        x_copies.append(remote(sums.at[2, :, at], xr.at[:, at], x_s.at[h], x_r.at[h], to_x))
    for c in x_copies:
        c.start()
    top(2)
    top(3)

    def middle(g):
        for n in range(3):
            z_copy(g, n).wait_recv()

        def one(i, _):
            x = zr[g, i].reshape(coarse, 2 * coarse)
            v = product_left(w_f2[...], jnp.concatenate([x, times_i(x)], axis=0))
            k = g * (k_own // GROUPS) + i
            gr, gi = gb[0, k].reshape(coarse, coarse), gb[1, k].reshape(coarse, coarse)
            vr, vi = v[:, :coarse], v[:, coarse:]
            w = jnp.concatenate([vr * gr - vi * gi, vr * gi + vi * gr], axis=1)
            u = product_left(w_inv[...], jnp.concatenate([w, times_i(w)], axis=0))
            s4[:, :, k] = u.reshape(s4.shape[0], s4.shape[1], ROWS, 2 * coarse)
            return 0

        lax.fori_loop(0, k_own // GROUPS, one, 0)

    def z_slice(h, src):
        return cz.at[:, pl.ds(h * rows_h, rows_h), src]

    def zc_copy(h, kind):
        src = z_peer[1] if kind == 2 else z
        where = to_z[1] if kind == 0 else to_z[0]
        return remote(z_slice(h, src), z_slice(h, src), zc_s.at[kind, h], zc_r.at[kind, h], where)

    def ratio(h):
        x_copies[h].wait_recv()
        for r in range(h * rows_h, (h + 1) * rows_h):
            nr = sums[0, 0, r] + xr[0, r]
            ni = sums[0, 1, r] + xr[1, r]
            d = sums[0, 2, r] + xr[2, r]
            cz[0, r, z] = nr / d
            cz[1, r, z] = ni / d
        zc_copy(h, 0).start()
        zc_copy(h, 1).start()

    tables[2].wait()
    tables[3].wait()
    tables[7].wait()
    green_copy.wait_recv()
    middle(0)
    for h in range(PARTS):
        ratio(h)
    middle(1)
    middle(2)
    for h in range(PARTS):
        zc_copy(h, 0).wait_recv()
        zc_copy(h, 2).start()
    middle(3)

    def zb_copy(j, n):
        return remote(
            s4.at[z_peer[n], j], fin.at[j, y, z], zb_s.at[j, n], zb_r.at[j, n], to_z[n]
        )

    own_copy = pltpu.make_async_copy(s4.at[z], fin.at[:, y, z], local_sem.at[0])
    own_copy.start()

    def send_z(j, _):
        for n in (2, 1, 0):
            zb_copy(j, n).start()
        return 0

    lax.fori_loop(0, f_chunks, send_z, 0)

    def piece(a, b, h):
        return cg.at[a, b, :, :, pl.ds(h * rows_h, rows_h)]

    def pass_on(a, b, h, sends, recvs, where):
        return remote(piece(a, b, h), piece(a, b, h), sends, recvs, where)

    def cy_copy(h):
        return pass_on(y, t, h, cy_s.at[h], cy_r.at[h], to_y)

    def cx_copy(n, h):
        return pass_on((y, oy)[n], t, h, cx_s.at[n, h], cx_r.at[n, h], to_x)

    def cc_copy(n, h):
        return pass_on((y, oy)[n % 2], (t, far)[n // 2], h, cc_s.at[n, h], cc_r.at[n, h], to_core)

    tables[4].wait()
    half = cg.shape[2] * ROWS

    def refine(h):
        zc_copy(h, 1).wait_recv()
        zc_copy(h, 2).wait_recv()
        for r in range(h * rows_h, (h + 1) * rows_h):
            x = jnp.concatenate([cz[0, r].reshape(coarse, coarse), cz[1, r].reshape(coarse, coarse)], axis=0)
            out = product_left(w_mid[...], x)
            for c in range(2):
                cg[y, t, :, c, r] = out[c * half : (c + 1) * half].reshape(cg.shape[2], ROWS, coarse)
        cy_copy(h).start()
        cx_copy(0, h).start()
        cc_copy(0, h).start()

    for h in range(PARTS):
        refine(h)

    def yh_copy(j):
        return remote(fin.at[j, y], fin.at[j, y], yh_s.at[j], yh_r.at[j], to_y)

    def out_copy(target, j, slot):
        return pltpu.make_async_copy(
            st.at[slot], target.at[:, pl.ds(j * ROWS, ROWS), :], out_sem.at[slot]
        )

    def emit(out, slot, s):
        st[slot, :, s, pl.ds(0, coarse)] = out[:f1]
        st[slot, :, s, pl.ds(coarse, coarse)] = out[f1:]

    def first_spec(j, slot):
        for s in range(ROWS):
            x = fin[j, :, :, :, s, :].reshape(coarse, 2 * coarse)
            emit(product_left(w_first[...], x, NT), slot, s)
        out_copy(ts_out, j, slot).start()

    def first_contrast(j, slot):
        for s in range(ROWS):
            x = cg[:, :, j, :, :, s, :].reshape(2 * coarse, coarse)
            emit(product_left(w_fc[...], x), slot, s)
        out_copy(tc_out, j, slot).start()

    own_copy.wait()
    tables[5].wait()
    tables[6].wait()
    lag = 2

    def forward(j, _):
        for n in range(3):
            zb_copy(j, n).wait_recv()
        yh_copy(j).start()

        @pl.when(j == 1)
        def _():
            for h in range(PARTS):
                cy_copy(h).wait_recv()
                cx_copy(1, h).start()
                cc_copy(1, h).start()

        @pl.when(j == 3)
        def _():
            for h in range(PARTS):
                cx_copy(0, h).wait_recv()
                cc_copy(2, h).start()

        @pl.when(j == 5)
        def _():
            for h in range(PARTS):
                cx_copy(1, h).wait_recv()
                cc_copy(3, h).start()

        @pl.when(j >= lag)
        def _():
            yh_copy(j - lag).wait_recv()

            @pl.when(j > lag)
            def _():
                out_copy(ts_out, j - lag - 1, 0).wait()

            first_spec(j - lag, 0)

        return 0

    lax.fori_loop(0, f_chunks, forward, 0)

    for h in range(PARTS):
        for n in range(4):
            cc_copy(n, h).wait_recv()

    def contrast_step(j, _):
        @pl.when(j > 0)
        def _():
            out_copy(tc_out, j - 1, 1).wait()

        first_contrast(j, 1)
        return 0

    lax.fori_loop(0, f_chunks, contrast_step, 0)

    def tail(j, _):
        yh_copy(j).wait_recv()
        out_copy(ts_out, j - 1, 0).wait()
        first_spec(j, 0)
        return 0

    lax.fori_loop(f_chunks - lag, f_chunks, tail, 0)

    for c in y_copies + core_copies + x_copies + [green_copy]:
        c.wait_send()
    for g in range(GROUPS):
        for n in range(3):
            z_copy(g, n).wait_send()
    for h in range(PARTS):
        for n in range(3):
            zc_copy(h, n).wait_send()
        cy_copy(h).wait_send()
        for n in range(2):
            cx_copy(n, h).wait_send()
        for n in range(4):
            cc_copy(n, h).wait_send()

    def drain(j, _):
        for n in range(3):
            zb_copy(j, n).wait_send()
        yh_copy(j).wait_send()
        return 0

    lax.fori_loop(0, f_chunks, drain, 0)
    out_copy(tc_out, f_chunks - 1, 1).wait()
    out_copy(ts_out, f_chunks - 1, 0).wait()


def last_body(m3_ref, m3c_ref, ts_ref, tc_ref, c_ref, o_ref):
    f1, rows, wide = ts_ref.shape
    fine = m3_ref.shape[1] // 2
    step = max(1, 256 // rows)
    for b in range(0, f1, step):
        at = slice(b, b + step)
        d = product_right(ts_ref[at].reshape(step * rows, wide), m3_ref[...])
        c = product_right(tc_ref[at].reshape(step * rows, wide), m3c_ref[...])
        dr, di, cr, ci = d[:, :fine], d[:, fine:], c[:, :fine], c[:, fine:]
        shape = (step, rows, fine)
        c_ref[0, at] = cr.reshape(shape)
        c_ref[1, at] = ci.reshape(shape)
        o_ref[0, 0, at] = (cr * dr - ci * di).reshape(shape)
        o_ref[0, 1, at] = (cr * di + ci * dr).reshape(shape)


def fused_device(tx, py, pz, fields, sources, green):
    coarse = fields.shape[4]
    fine = 2 * coarse
    many = fields.shape[0]
    x1, x2 = fields.shape[2], fields.shape[3]
    f1, f2 = fine // py, fine // pz
    lanes = 2 * x1
    part = x1 // tx
    k3 = coarse // pz
    k_own = k3 // py
    k_group = k_own // GROUPS
    x_chunks, f_chunks = x2 // ROWS, f2 // ROWS

    fwd, inv = forward_matrix(coarse), inverse_matrix(coarse, fine)
    refined = inv @ fwd
    ri = lambda m: np.concatenate([m.real, m.imag], axis=1)
    grid = np.arange(coarse).reshape(pz, py, GROUPS, k_group)
    rows_s1 = grid.transpose(1, 2, 0, 3).reshape(-1)
    rows_k3 = grid.transpose(1, 0, 2, 3).reshape(-1)
    h_s1 = left_table(ri(fwd)[rows_s1])
    top = block_form(fwd).reshape(2 * coarse, 2, py, x1).transpose(2, 1, 3, 0)
    h_top = right_table(
        np.stack([top[[q, 1 - q]].reshape(2 * coarse, 2 * coarse) for q in range(py)])
    )
    h_f2 = left_table(ri(fwd))
    h_inv = left_table(ri(inv))
    first = block_form(inv).reshape(2, py, f1, 2 * coarse).transpose(1, 0, 2, 3)
    h_first = left_table(first.reshape(py, 2 * f1, 2 * coarse))
    mid = block_form(refined).reshape(2, pz, f2, 2 * coarse).transpose(1, 0, 2, 3)
    h_mid = left_table(mid.reshape(pz, 2 * f2, 2 * coarse))
    fc = block_form(refined).reshape(2, py, f1, 2, py, tx, part).transpose(1, 0, 2, 4, 5, 3, 6)
    h_fc = left_table(fc.reshape(py, 2 * f1, 2 * coarse))
    last = block_form(inv).transpose(2, 3, 0, 1)[:, rows_k3].reshape(2 * coarse, 2 * fine)
    last_c = block_form(refined).transpose(2, 3, 0, 1).reshape(2 * coarse, 2 * fine)
    m3, m3c = right_table(last), right_table(last_c)

    vm = lambda *dims: pltpu.VMEM(dims, F32)
    wm = lambda *dims: pltpu.VMEM(dims, BF16)
    dma = lambda *dims: pltpu.SemaphoreType.DMA(dims)
    pair = lambda *dims: [dma(*dims), dma(*dims)]
    wide = 2 * coarse
    scratch = [
        vm(x_chunks, 2, x1, ROWS, coarse),
        vm(py, GROUPS, pz * k_group, x_chunks, ROWS, lanes),
        vm(GROUPS, pz * k_group, x_chunks, ROWS, lanes),
        vm(GROUPS, pz, k_group, x2, wide),
        vm(GROUPS, k_group, pz, x2, wide),
        vm(2, k_own, py, coarse // py, coarse),
        vm(pz, f_chunks, k_own, ROWS, wide),
        vm(f_chunks, py, pz, k_own, ROWS, wide),
        vm(2, many, 2, ROWS, x2, coarse),
        vm(2, many, 2, ROWS, x2, coarse),
        vm(tx, 3, part, x2, coarse),
        vm(2, 3, part, x2, coarse),
        vm(3, part, x2, coarse),
        vm(2, part, pz, x2, coarse),
        vm(py, tx, f_chunks, 2, part, ROWS, coarse),
        vm(2, f1, ROWS, wide),
        wm(*h_s1.shape), wm(*h_top.shape[1:]), wm(*h_f2.shape), wm(*h_inv.shape),
        wm(*h_first.shape[1:]), wm(*h_mid.shape[1:]), wm(*h_fc.shape[1:]),
        dma(x_chunks + 8), dma(2, 2), dma(2), dma(1),
        *pair(GROUPS), *pair(GROUPS, 3), *pair(1), *pair(2), *pair(PARTS), *pair(3, PARTS),
        *pair(PARTS), *pair(2, PARTS), *pair(4, PARTS), *pair(f_chunks, 3), *pair(f_chunks),
    ]
    middle_shape = jax.ShapeDtypeStruct((f1, f2, wide), F32)
    operands = (fields, sources, green, h_s1, h_top, h_f2, h_inv, h_first, h_mid, h_fc)
    anywhere = pl.BlockSpec(memory_space=pl.ANY)
    ts, tc = pl.pallas_call(
        exchange_body,
        in_specs=[anywhere] * len(operands),
        out_specs=[anywhere] * 2,
        out_shape=[middle_shape] * 2,
        scratch_shapes=scratch,
        name="exchange",
        compiler_params=pltpu.CompilerParams(
            collective_id=0, has_side_effects=True, vmem_limit_bytes=63 * 2**20
        ),
    )(*operands)

    blocked = pl.BlockSpec((f1, ROWS, wide), lambda i: (0, i, 0))
    whole = pl.BlockSpec(m3.shape, lambda i: (0, 0))
    return pl.pallas_call(
        last_body,
        grid=(f_chunks,),
        in_specs=[whole, whole, blocked, blocked],
        out_specs=[
            pl.BlockSpec((2, f1, ROWS, fine), lambda i: (0, 0, i, 0)),
            pl.BlockSpec((1, 2, f1, ROWS, fine), lambda i: (0, 0, 0, i, 0)),
        ],
        out_shape=[
            jax.ShapeDtypeStruct((2, f1, f2, fine), F32),
            jax.ShapeDtypeStruct((1, 2, f1, f2, fine), F32),
        ],
        name="last",
        compiler_params=pltpu.CompilerParams(vmem_limit_bytes=48 * 2**20),
    )(m3, m3c, ts, tc)


def fourier_matrix(out_index, in_index, period, exponent_sign, weight):
    phases = out_index[:, None] * in_index[None, :] % period
    angles = exponent_sign * 2.0 * math.pi / period * phases.astype(jnp.float32)
    cosine = weight * jnp.cos(angles)
    sine_part = weight * jnp.sin(angles)
    return jnp.stack([jnp.stack([cosine, -sine_part], 1), jnp.stack([sine_part, cosine], 1)], 0)


def local_step(values, matrix):
    return jnp.einsum("fcxyl,dkcl->fdyxk", values, matrix, precision=lax.Precision.HIGHEST)


def remote_step(values, matrix):
    return jnp.einsum("fclxy,dkcl->fdxyk", values, matrix, precision=lax.Precision.HIGHEST)


def turn(values, matrix, axis):
    return remote_step(lax.all_to_all(values, axis, split_axis=4, concat_axis=2, tiled=True), matrix)


def forward_pass(values, matrix):
    return turn(turn(local_step(values, matrix), matrix, "pz"), matrix, "py")


def inverse_pass(values, matrix):
    return turn(turn(local_step(values, matrix), matrix, "py"), matrix, "pz")


def complex_product(first_factor, second_factor):
    real_part = first_factor[0] * second_factor[0] - first_factor[1] * second_factor[1]
    imag_part = first_factor[0] * second_factor[1] + first_factor[1] * second_factor[0]
    return jnp.stack([real_part, imag_part])


def general_device(fields, sources, green):
    coarse = fields.shape[4]
    fine = 2 * coarse
    index = jnp.arange(coarse, dtype=jnp.int32)
    fine_index = jnp.arange(fine, dtype=jnp.int32)
    signed_coarse = jnp.where(index < coarse // 2, index, index - coarse)
    unit_coarse = jnp.ones((coarse, 1), F32)
    unit_fine = jnp.ones((fine, 1), F32)
    coarse_forward = fourier_matrix(index, index, coarse, -1.0, unit_coarse)
    padded_inverse = fourier_matrix(fine_index, signed_coarse, fine, 1.0, unit_fine / coarse)
    fr, fi, sr, si = fields[:, 0], fields[:, 1], sources[:, 0], sources[:, 1]
    numer_re = jnp.sum(sr * fr + si * fi, axis=0)
    numer_im = jnp.sum(si * fr - sr * fi, axis=0)
    denom = jnp.sum(fr * fr + fi * fi, axis=0)
    numer_re, numer_im, denom = lax.psum((numer_re, numer_im, denom), "tx")
    contrast = jnp.stack([numer_re / denom, numer_im / denom])[None]
    contrast_fine = inverse_pass(forward_pass(contrast, coarse_forward), padded_inverse)[0]
    spectrum = forward_pass(sources[0:1], coarse_forward)
    weighted = complex_product(spectrum[0], green)[None]
    domain_field = inverse_pass(weighted, padded_inverse)[0]
    return contrast_fine, complex_product(contrast_fine, domain_field)[None]


def solution(mesh):
    tx, py, pz = mesh.shape["tx"], mesh.shape["py"], mesh.shape["pz"]

    def on_device(fields, sources, green):
        x1, x2, coarse = fields.shape[2:]
        fused = (
            tx == 4 and py == 2 and pz == 4
            and coarse % 128 == 0 and (2 * x1) % 128 == 0 and x1 % (tx * ROWS) == 0
            and x2 % ROWS == 0 and (2 * coarse // pz) % ROWS == 0
            and coarse % (pz * py * GROUPS) == 0 and x1 % (tx * PARTS) == 0
            and coarse * coarse * coarse <= 2**21
        )
        if fused:
            return fused_device(tx, py, pz, fields, sources, green)
        return general_device(fields, sources, green)

    placed = (
        P("tx", None, "py", "pz", None),
        P("tx", None, "py", "pz", None),
        P(None, "pz", "py", None),
    )
    return jax.shard_map(
        on_device,
        mesh=mesh,
        in_specs=placed,
        out_specs=(P(None, "py", "pz", None), P("tx", None, "py", "pz", None)),
        check_vma=False,
    )
```

profile of v0, /device:TPU:0, one launch (start us, length us, event | category | flops | bytes accessed | tf_op | source)
XLA Modules:
  0.0 261.5 jit_solution(16848710468739930246)
XLA Ops:
  0.6 0.0 copy-start
  0.6 237.3 %exchange.1 = (f32[128,64,256]{2,1,0:T(8,128)}, f32[128,64,256]{2,1,0:T(8,128)}) custom-call(f32[4,2,64,32,128]{4,3,2,1,0:T(8,128)} %fields.1, f32[4,2,64,32,128]{4,3,2,1,0:T(8,128)} %sources.1, f32[2,32,64,128]{3,2,1,0:T(8,128)} %green.1, bf16[128,768]{1,0:T(8,128)(2,1)} %constant.18.clone.h_s1, bf16[2,768,256]{2,1,0:T(8,128)(2,1)} %constant.19.clone.h_top, ...), custom_call_target="tpu_custom_call" | custom-call | tf_op jit(solution)/shard_map/exchange/pallas_call | solution.py:559
  238.0 0.0 copy-done
  238.0 0.0 copy-start.1
  238.0 1.1 copy-done.1
  239.1 22.4 %last.1 = (f32[2,128,64,256]{3,2,1,0:T(8,128)}, f32[1,2,128,64,256]{4,3,2,1,0:T(8,128)}) custom-call(bf16[768,512]{1,0:T(8,128)(2,1)S(1)} %copy-done.1, bf16[768,512]{1,0:T(8,128)(2,1)S(1)} %copy-done, f32[128,64,256]{2,1,0:T(8,128)} %get-tuple-element.4.ts_ref, f32[128,64,256]{2,1,0:T(8,128)} %get-tuple-element.5.tc_ref), custom_call_target="tpu_custom_call" | custom-call | tf_op jit(solution)/shard_map/last/pallas_call | solution.py:573
Async XLA Ops:
  0.6 237.3 %copy-start = (bf16[768,512]{1,0:T(8,128)(2,1)S(1)}, bf16[768,512]{1,0:T(8,128)(2,1)}, u32[]{:S(2)}) copy-start(bf16[768,512]{1,0:T(8,128)(2,1)} %constant.26.clone.m3c_ref) | copy-start | bytes 2359300
  238.0 1.1 copy-start.1
where the time goes:
time: 262 us; the launch traced here: 261 us
  Pallas kernels  260 us (99%)
    pallas_call x1, Pallas kernels, fused_device(): pl.pallas_call(exchange_body, in_specs=[anywhere] * len(operands), out_sp...  237 us
    pallas_call x1, Pallas kernels, fused_device(): pl.pallas_call(last_body, grid=(f_chunks,), in_specs=[whole, whole, block...  22.4 us

commit v1 on v0

--- a/solution.py
+++ b/solution.py
@@ -162,7 +162,6 @@
     peers = to_z + [to_y, to_core, to_x]
     for where in peers:
         pl.semaphore_signal(barrier, inc=1, device_id=where, device_id_type=MESH)
-    pl.semaphore_wait(barrier, len(peers))
 
     tables[0].wait()
     for c in loads:
@@ -179,6 +178,7 @@
         return 0
 
     lax.fori_loop(0, x_chunks, depth, 0)
+    pl.semaphore_wait(barrier, len(peers))
 
     y_copies = [remote(s1.at[oy, g], yr.at[g], y_s.at[g], y_r.at[g], to_y) for g in range(GROUPS)]
     for c in y_copies:
@@ -261,10 +261,11 @@
     top(2)
     top(3)
 
-    def middle(g):
+    def arrive(g):
         for n in range(3):
             z_copy(g, n).wait_recv()
 
+    def middle(g):
         def one(i, _):
             x = zr[g, i].reshape(coarse, 2 * coarse)
             v = product_left(w_f2[...], jnp.concatenate([x, times_i(x)], axis=0))
@@ -296,35 +297,6 @@
             cz[1, r, z] = ni / d
         zc_copy(h, 0).start()
         zc_copy(h, 1).start()
-
-    tables[2].wait()
-    tables[3].wait()
-    tables[7].wait()
-    green_copy.wait_recv()
-    middle(0)
-    for h in range(PARTS):
-        ratio(h)
-    middle(1)
-    middle(2)
-    for h in range(PARTS):
-        zc_copy(h, 0).wait_recv()
-        zc_copy(h, 2).start()
-    middle(3)
-
-    def zb_copy(j, n):
-        return remote(
-            s4.at[z_peer[n], j], fin.at[j, y, z], zb_s.at[j, n], zb_r.at[j, n], to_z[n]
-        )
-
-    own_copy = pltpu.make_async_copy(s4.at[z], fin.at[:, y, z], local_sem.at[0])
-    own_copy.start()
-
-    def send_z(j, _):
-        for n in (2, 1, 0):
-            zb_copy(j, n).start()
-        return 0
-
-    lax.fori_loop(0, f_chunks, send_z, 0)
 
     def piece(a, b, h):
         return cg.at[a, b, :, :, pl.ds(h * rows_h, rows_h)]
@@ -356,8 +328,50 @@
         cx_copy(0, h).start()
         cc_copy(0, h).start()
 
+    cut = k_own - k_own // GROUPS
+    early = 2
+
+    def zb_copy(j, h, n):
+        ks = pl.ds(0, cut) if h == 0 else pl.ds(cut, k_own - cut)
+        return remote(
+            s4.at[z_peer[n], j, ks], fin.at[j, y, z, ks],
+            zb_s.at[j, h, n], zb_r.at[j, h, n], to_z[n],
+        )
+
+    def send_z(j, h):
+        for n in (2, 1, 0):
+            zb_copy(j, h, n).start()
+
+    for h in range(PARTS):
+        ratio(h)
+    for n in (2, 3, 7):
+        tables[n].wait()
+    green_copy.wait_recv()
+    for g in (0, 1):
+        arrive(g)
+        middle(g)
+    for h in range(PARTS):
+        zc_copy(h, 0).wait_recv()
+        zc_copy(h, 2).start()
+    arrive(2)
+    middle(2)
     for h in range(PARTS):
         refine(h)
+    arrive(3)
+    for j in range(early):
+        send_z(j, 0)
+    middle(3)
+    own_copy = pltpu.make_async_copy(s4.at[z], fin.at[:, y, z], local_sem.at[0])
+    own_copy.start()
+    for j in range(early):
+        send_z(j, 1)
+
+    def send_rest(j, _):
+        send_z(j, 0)
+        send_z(j, 1)
+        return 0
+
+    lax.fori_loop(early, f_chunks, send_rest, 0)
 
     def yh_copy(j):
         return remote(fin.at[j, y], fin.at[j, y], yh_s.at[j], yh_r.at[j], to_y)
@@ -388,25 +402,34 @@
     tables[6].wait()
     lag = 2
 
+    def contrast_step(j, _):
+        @pl.when(j > 0)
+        def _():
+            out_copy(tc_out, j - 1, 1).wait()
+
+        first_contrast(j, 1)
+        return 0
+
     def forward(j, _):
-        for n in range(3):
-            zb_copy(j, n).wait_recv()
+        for h in range(2):
+            for n in range(3):
+                zb_copy(j, h, n).wait_recv()
         yh_copy(j).start()
 
-        @pl.when(j == 1)
+        @pl.when(j == 0)
         def _():
             for h in range(PARTS):
                 cy_copy(h).wait_recv()
                 cx_copy(1, h).start()
                 cc_copy(1, h).start()
 
-        @pl.when(j == 3)
+        @pl.when(j == 1)
         def _():
             for h in range(PARTS):
                 cx_copy(0, h).wait_recv()
                 cc_copy(2, h).start()
 
-        @pl.when(j == 5)
+        @pl.when(j == 3)
         def _():
             for h in range(PARTS):
                 cx_copy(1, h).wait_recv()
@@ -422,23 +445,20 @@
 
             first_spec(j - lag, 0)
 
+        @pl.when(j == f_chunks // 2)
+        def _():
+            for h in range(PARTS):
+                for n in range(4):
+                    cc_copy(n, h).wait_recv()
+
+        @pl.when(j >= f_chunks // 2)
+        def _():
+            at = 2 * (j - f_chunks // 2)
+            lax.fori_loop(at, at + 2, contrast_step, 0)
+
         return 0
 
     lax.fori_loop(0, f_chunks, forward, 0)
-
-    for h in range(PARTS):
-        for n in range(4):
-            cc_copy(n, h).wait_recv()
-
-    def contrast_step(j, _):
-        @pl.when(j > 0)
-        def _():
-            out_copy(tc_out, j - 1, 1).wait()
-
-        first_contrast(j, 1)
-        return 0
-
-    lax.fori_loop(0, f_chunks, contrast_step, 0)
 
     def tail(j, _):
         yh_copy(j).wait_recv()
@@ -463,8 +483,9 @@
             cc_copy(n, h).wait_send()
 
     def drain(j, _):
-        for n in range(3):
-            zb_copy(j, n).wait_send()
+        for h in range(2):
+            for n in range(3):
+                zb_copy(j, h, n).wait_send()
         yh_copy(j).wait_send()
         return 0
 
@@ -551,7 +572,7 @@
         wm(*h_first.shape[1:]), wm(*h_mid.shape[1:]), wm(*h_fc.shape[1:]),
         dma(x_chunks + 8), dma(2, 2), dma(2), dma(1),
         *pair(GROUPS), *pair(GROUPS, 3), *pair(1), *pair(2), *pair(PARTS), *pair(3, PARTS),
-        *pair(PARTS), *pair(2, PARTS), *pair(4, PARTS), *pair(f_chunks, 3), *pair(f_chunks),
+        *pair(PARTS), *pair(2, PARTS), *pair(4, PARTS), *pair(f_chunks, 2, 3), *pair(f_chunks),
     ]
     middle_shape = jax.ShapeDtypeStruct((f1, f2, wide), F32)
     operands = (fields, sources, green, h_s1, h_top, h_f2, h_inv, h_first, h_mid, h_fc)
@@ -652,7 +673,7 @@
         fused = (
             tx == 4 and py == 2 and pz == 4
             and coarse % 128 == 0 and (2 * x1) % 128 == 0 and x1 % (tx * ROWS) == 0
-            and x2 % ROWS == 0 and (2 * coarse // pz) % ROWS == 0
+            and x2 % ROWS == 0 and (2 * coarse // pz) % (2 * ROWS) == 0 and 2 * coarse // pz >= 8 * ROWS
             and coarse % (pz * py * GROUPS) == 0 and x1 % (tx * PARTS) == 0
             and coarse * coarse * coarse <= 2**21
         )

time: 262 us -> 254 us (0.969)
  Pallas kernels: 260 us -> 252 us
    pallas_call x1, Pallas kernels: 237 us -> 229 us  [fused_device(): pl.pallas_call(exchange_body, in_specs=[anywhere] * len(operands), out_sp...]
where the time goes in v1:
time: 254 us
  Pallas kernels  252 us (99%)
    pallas_call x1, Pallas kernels, fused_device(): pl.pallas_call(exchange_body, in_specs=[anywhere] * len(operands), out_sp...  229 us
    pallas_call x1, Pallas kernels, fused_device(): pl.pallas_call(last_body, grid=(f_chunks,), in_specs=[whole, whole, block...  22.4 us

profile of v1, /device:TPU:0, one launch (start us, length us, event | category | flops | bytes accessed | tf_op | source)
XLA Modules:
  0.0 253.5 jit_solution(16054445952985963184)
XLA Ops:
  0.6 0.0 copy-start
  0.6 229.4 %exchange.1 = (f32[128,64,256]{2,1,0:T(8,128)}, f32[128,64,256]{2,1,0:T(8,128)}) custom-call(f32[4,2,64,32,128]{4,3,2,1,0:T(8,128)} %fields.1, f32[4,2,64,32,128]{4,3,2,1,0:T(8,128)} %sources.1, f32[2,32,64,128]{3,2,1,0:T(8,128)} %green.1, bf16[128,768]{1,0:T(8,128)(2,1)} %constant.18.clone.h_s1, bf16[2,768,256]{2,1,0:T(8,128)(2,1)} %constant.19.clone.h_top, ...), custom_call_target="tpu_custom_call" | custom-call | tf_op jit(solution)/shard_map/exchange/pallas_call | solution.py:580
  230.0 0.0 copy-done
  230.0 0.0 copy-start.1
  230.1 1.1 copy-done.1
  231.2 22.4 %last.1 = (f32[2,128,64,256]{3,2,1,0:T(8,128)}, f32[1,2,128,64,256]{4,3,2,1,0:T(8,128)}) custom-call(bf16[768,512]{1,0:T(8,128)(2,1)S(1)} %copy-done.1, bf16[768,512]{1,0:T(8,128)(2,1)S(1)} %copy-done, f32[128,64,256]{2,1,0:T(8,128)} %get-tuple-element.4.ts_ref, f32[128,64,256]{2,1,0:T(8,128)} %get-tuple-element.5.tc_ref), custom_call_target="tpu_custom_call" | custom-call | tf_op jit(solution)/shard_map/last/pallas_call | solution.py:594
Async XLA Ops:
  0.6 229.4 %copy-start = (bf16[768,512]{1,0:T(8,128)(2,1)S(1)}, bf16[768,512]{1,0:T(8,128)(2,1)}, u32[]{:S(2)}) copy-start(bf16[768,512]{1,0:T(8,128)(2,1)} %constant.26.clone.m3c_ref) | copy-start | bytes 2359300
  230.0 1.1 copy-start.1

commit v2 on v1

--- a/solution.py
+++ b/solution.py
@@ -226,9 +226,11 @@
         other = yr[g].reshape(rows, lanes)
         out = product_right(jnp.concatenate([own, other], axis=1), w_top[...])
         s2[g] = out.reshape(s2.shape[1:])
+        zr[g, :, z] = s2[g, z]
+
+    def send_top(g):
         for n in (2, 1, 0):
             z_copy(g, n).start()
-        zr[g, :, z] = s2[g, z]
 
     sum_block(0)
     core_copies[0].start()
@@ -236,12 +238,14 @@
     core_copies[1].start()
     tables[1].wait()
     top(0)
+    send_top(0)
     green_copy = remote(
         green.at[:, pl.ds(oy * k_own, k_own)], gb.at[:, :, y], g_s.at[0], g_r.at[0], to_y
     )
     sum_block(2)
     sum_block(3)
     top(1)
+    send_top(1)
     green_copy.start()
     for n, j in enumerate((0, 2)):
         core_copies[n].wait_recv()
@@ -344,6 +348,7 @@
 
     for h in range(PARTS):
         ratio(h)
+    send_top(2)
     for n in (2, 3, 7):
         tables[n].wait()
     green_copy.wait_recv()
@@ -353,13 +358,14 @@
     for h in range(PARTS):
         zc_copy(h, 0).wait_recv()
         zc_copy(h, 2).start()
+    send_top(3)
     arrive(2)
     middle(2)
+    for j in range(early):
+        send_z(j, 0)
     for h in range(PARTS):
         refine(h)
     arrive(3)
-    for j in range(early):
-        send_z(j, 0)
     middle(3)
     own_copy = pltpu.make_async_copy(s4.at[z], fin.at[:, y, z], local_sem.at[0])
     own_copy.start()

time: 254 us -> 249 us (0.980)
  Pallas kernels: 252 us -> 247 us
    pallas_call x1, Pallas kernels: 229 us -> 225 us  [fused_device(): pl.pallas_call(exchange_body, in_specs=[anywhere] * len(operands), out_sp...]
where the time goes in v2:
time: 249 us
  Pallas kernels  247 us (99%)
    pallas_call x1, Pallas kernels, fused_device(): pl.pallas_call(exchange_body, in_specs=[anywhere] * len(operands), out_sp...  225 us
    pallas_call x1, Pallas kernels, fused_device(): pl.pallas_call(last_body, grid=(f_chunks,), in_specs=[whole, whole, block...  22.4 us

profile of v2, /device:TPU:0, one launch (start us, length us, event | category | flops | bytes accessed | tf_op | source)
XLA Modules:
  0.0 248.7 jit_solution(10227288047465082447)
XLA Ops:
  0.6 0.0 copy-start
  0.6 224.5 %exchange.1 = (f32[128,64,256]{2,1,0:T(8,128)}, f32[128,64,256]{2,1,0:T(8,128)}) custom-call(f32[4,2,64,32,128]{4,3,2,1,0:T(8,128)} %fields.1, f32[4,2,64,32,128]{4,3,2,1,0:T(8,128)} %sources.1, f32[2,32,64,128]{3,2,1,0:T(8,128)} %green.1, bf16[128,768]{1,0:T(8,128)(2,1)} %constant.18.clone.h_s1, bf16[2,768,256]{2,1,0:T(8,128)(2,1)} %constant.19.clone.h_top, ...), custom_call_target="tpu_custom_call" | custom-call | tf_op jit(solution)/shard_map/exchange/pallas_call | solution.py:586
  225.2 0.0 copy-done
  225.2 0.0 copy-start.1
  225.2 1.1 copy-done.1
  226.3 22.4 %last.1 = (f32[2,128,64,256]{3,2,1,0:T(8,128)}, f32[1,2,128,64,256]{4,3,2,1,0:T(8,128)}) custom-call(bf16[768,512]{1,0:T(8,128)(2,1)S(1)} %copy-done.1, bf16[768,512]{1,0:T(8,128)(2,1)S(1)} %copy-done, f32[128,64,256]{2,1,0:T(8,128)} %get-tuple-element.4.ts_ref, f32[128,64,256]{2,1,0:T(8,128)} %get-tuple-element.5.tc_ref), custom_call_target="tpu_custom_call" | custom-call | tf_op jit(solution)/shard_map/last/pallas_call | solution.py:600
Async XLA Ops:
  0.6 224.5 %copy-start = (bf16[768,512]{1,0:T(8,128)(2,1)S(1)}, bf16[768,512]{1,0:T(8,128)(2,1)}, u32[]{:S(2)}) copy-start(bf16[768,512]{1,0:T(8,128)(2,1)} %constant.26.clone.m3c_ref) | copy-start | bytes 2359300
  225.2 1.1 copy-start.1
